TPU v7x, 32 devices: a whole 2x2x4 slice. The times are simulated.
32 devices in a mesh: replica: 4 (over y, core), kvhead: 4 (over z), ffn: 2 (over x).
Axes of the slice: x: 2, y: 2, z: 4, core: 2. Of those that a mesh axis runs over, the one named last changes fastest.
Arguments:
- queries: bfloat16 [16, 16384], P('replica', 'kvhead'), may hold values from -400 to 400
- k_cache: bfloat16 [512, 64, 1024], P(('replica', 'ffn'), None, 'kvhead'), may hold values from -6 to 6
- v_cache: bfloat16 [512, 64, 1024], P(('replica', 'ffn'), None, 'kvhead'), may hold values from -6 to 6
- page_table: int32 [16, 32], P('replica', 'ffn'), may hold values from 0 to 63, as said below
- seq_lens: int32 [16], P('replica'), may hold values from 1 to 2048, as said below
- out_proj: bfloat16 [16384, 16384], P('kvhead', ('replica', 'ffn')), may hold values from -0.125 to 0.125
- residual: bfloat16 [16, 16384], P('kvhead', ('replica', 'ffn')), may hold values from -40 to 40
- norm_gain: bfloat16 [16384], P(('replica', 'ffn')), may hold values from 0.099609375 to 1.8984375
- gate_weight: bfloat16 [26624, 16384], P(('replica', 'kvhead', 'ffn')), may hold values from -0.046875 to 0.046875
- up_weight: bfloat16 [26624, 16384], P(('replica', 'kvhead', 'ffn')), may hold values from -0.046875 to 0.046875
Outputs:
- post_attn: bfloat16 [16, 16384], P('kvhead', ('replica', 'ffn'))
- hidden: bfloat16 [16, 26624], P(None, ('replica', 'kvhead', 'ffn'))
Inputs may be any that keep to these rules, and one draw needn't show every extreme that they name: `page_table`: over the 4 rows of one replica, the entries of page columns j with the same j // 16 name every pool page 0 to 63 exactly once. `seq_lens`: some row has length 2048.
All inputs are finite; a program needn't handle non-finite values.
Results may differ from a plain program's by a relative error of at most 0.0079.
Values may be sent and summed in bfloat16 or wider, within the bound.
A program may use at most 192 MiB of HBM per device.

v0:
```python
import math
import jax
import jax.numpy as jnp
from jax import lax
from jax.sharding import PartitionSpec as P

D = 16384
HD = 128
GQ = 16
NEG_FILL = -1e30
NORM_EPS = 1e-05


def merged(part, axis, combine):
    gathered = jax.tree.map(lambda a: lax.all_gather(a, axis), part)

    def take(source):
        return jax.tree.map(lambda a: lax.dynamic_index_in_dim(a, source, 0, False), gathered)

    return lax.fori_loop(
        1, lax.axis_size(axis), lambda source, state: combine(state, take(source)), take(0)
    )


def join_parts(earlier, later):
    first_max, first_total, first_out = earlier
    second_max, second_total, second_out = later
    overall = jnp.maximum(first_max, second_max)
    first_factor = jnp.exp(first_max - overall)
    second_factor = jnp.exp(second_max - overall)
    joined_total = first_total * first_factor + second_total * second_factor
    joined_out = first_out * first_factor[..., None] + second_out * second_factor[..., None]
    return (overall, joined_total, joined_out)


def per_device(
    queries,
    k_cache,
    v_cache,
    page_table,
    seq_lens,
    out_proj,
    residual,
    norm_gain,
    gate_weight,
    up_weight,
):
    score_scale = 1.0 / math.sqrt(HD)
    row_count = queries.shape[0]
    local_heads = k_cache.shape[2] // HD
    span_len = page_table.shape[1] * k_cache.shape[1]
    key_rows = k_cache[page_table].reshape(row_count, span_len, local_heads, HD)
    value_rows = v_cache[page_table].reshape(row_count, span_len, local_heads, HD)
    query_heads = queries.reshape(row_count, local_heads, GQ, HD)
    scores = (
        jnp.einsum("rkgd,rskd->rkgs", query_heads, key_rows, preferred_element_type=jnp.float32)
        * score_scale
    )
    positions = lax.axis_index("ffn") * span_len + jnp.arange(span_len, dtype=jnp.int32)
    visible = (positions[None, :] < seq_lens[:, None])[:, None, None, :]
    block_max = jnp.max(jnp.where(visible, scores, NEG_FILL), axis=-1)
    weights = jnp.where(visible, jnp.exp(scores - block_max[..., None]), 0.0)
    block_total = jnp.sum(weights, axis=-1)
    block_out = jnp.einsum(
        "rkgs,rskd->rkgd",
        weights.astype(jnp.bfloat16),
        value_rows,
        preferred_element_type=jnp.float32,
    )
    overall, denominator, weighted = merged((block_max, block_total, block_out), "ffn", join_parts)
    contexts = (
        (weighted / denominator[..., None])
        .astype(jnp.bfloat16)
        .reshape(row_count, local_heads * GQ * HD)
    )
    partial_value = jnp.dot(
        lax.all_gather(contexts, "replica", axis=0, tiled=True),
        out_proj,
        preferred_element_type=jnp.float32,
    )
    own_count = residual.shape[0]
    own_first = lax.axis_index("kvhead") * own_count
    own_part = lax.dynamic_slice_in_dim(partial_value, own_first, own_count, 0) + residual.astype(
        jnp.float32
    )
    partial_value = lax.dynamic_update_slice_in_dim(partial_value, own_part, own_first, 0)
    gain_wide = norm_gain.astype(jnp.float32)
    summed = lax.psum(partial_value, "kvhead")
    post_all = summed.astype(jnp.bfloat16)
    post_attn = lax.dynamic_slice_in_dim(post_all, own_first, own_count, 0)
    widened = post_all.astype(jnp.float32)
    squares = lax.psum(jnp.sum(widened * widened, axis=1), ("replica", "ffn"))
    normed = (widened * lax.rsqrt(squares / D + NORM_EPS)[:, None] * gain_wide).astype(jnp.bfloat16)
    contract = (((1,), (1,)), ((), ()))
    shard_cols = lax.all_gather(normed, ("replica", "ffn"), axis=1, tiled=True)
    gate_sum = lax.dot_general(
        shard_cols, gate_weight, contract, preferred_element_type=jnp.float32
    )
    up_sum = lax.dot_general(shard_cols, up_weight, contract, preferred_element_type=jnp.float32)
    hidden = (jax.nn.silu(gate_sum) * up_sum).astype(jnp.bfloat16)
    return (post_attn, hidden)


def solution(mesh):
    in_specs = (
        P("replica", "kvhead"),
        P(("replica", "ffn"), None, "kvhead"),
        P(("replica", "ffn"), None, "kvhead"),
        P("replica", "ffn"),
        P("replica"),
        P("kvhead", ("replica", "ffn")),
        P("kvhead", ("replica", "ffn")),
        P(("replica", "ffn")),
        P(("replica", "kvhead", "ffn"), None),
        P(("replica", "kvhead", "ffn"), None),
    )
    out_specs = (P("kvhead", ("replica", "ffn")), P(None, ("replica", "kvhead", "ffn")))
    return jax.shard_map(
        per_device, mesh=mesh, in_specs=in_specs, out_specs=out_specs, check_vma=False
    )
```

profile of v0, /device:TPU:1, one launch (start us, length us, event | category | flops | bytes accessed | tf_op | source)
XLA Modules:
  0.0 121.5 jit_solution(7688263210400951377)
XLA Ops:
  0.6 0.0 copy-start
  0.7 0.9 broadcast_compare_fusion
  1.5 0.7 compare_select_fusion
  2.2 0.1 reshape.100
  2.3 0.0 copy-done
  2.3 2.0 %gather_fusion = bf16[64,64,256]{2,1,0:T(8,128)(2,1)} fusion(bf16[64,64,256]{2,1,0:T(8,128)(2,1)S(1)} %copy-done, s32[1024]{0:T(1024)S(1)} %pad_clamp_fusion), kind=kCustom, calls=%fused_computation | custom fusion | bytes 4194560 | tf_op jit(solution)/shard_map/gather | solution.py:52
  4.4 2.6 %reshape.95 = bf16[4,1024,2,128]{3,2,1,0:T(2,128)(2,1)S(1)} reshape(bf16[64,64,256]{2,1,0:T(8,128)(2,1)} %gather_fusion) | data formatting | bytes 4194304 | tf_op jit(solution)/shard_map/reshape | solution.py:52
  6.9 0.0 copy-done.2
  6.9 0.7 select_reduce_fusion
  7.7 0.3 bitcast_reduce_fusion
  7.9 3.8 %all-gather.2 = f32[8,2,16]{2,1,0:T(2,128)S(1)} all-gather(f32[4,2,16]{2,1,0:T(2,128)S(1)} %bitcast_reduce_fusion), channel_id=4, replica_groups=mesh['replica'=4,'kvhead'=4,'ffn'=2] {'ffn'}, dimensions={0}, use_global_device_ids=true | all-gather | bytes 1536 | tf_op jit(solution)/shard_map/all_gather | solution.py:15
  11.7 3.2 %all-gather.1 = f32[8,2,16]{2,1,0:T(2,128)S(1)} all-gather(f32[4,2,16]{2,1,0:T(2,128)S(1)} %get-tuple-element.21), channel_id=3, replica_groups=mesh['replica'=4,'kvhead'=4,'ffn'=2] {'ffn'}, dimensions={0}, use_global_device_ids=true | all-gather | bytes 1536 | tf_op jit(solution)/shard_map/all_gather | solution.py:15
  14.9 2.3 %gather_fusion.1 = bf16[64,64,256]{2,1,0:T(8,128)(2,1)S(1)} fusion(bf16[64,64,256]{2,1,0:T(8,128)(2,1)} %param.12, s32[1024]{0:T(1024)S(1)} %pad_clamp_fusion), kind=kCustom, calls=%fused_computation.1 | custom fusion | bytes 4194560 | tf_op jit(solution)/shard_map/gather | solution.py:53
  17.2 2.1 %reshape.97 = bf16[4,1024,2,128]{3,2,1,0:T(2,128)(2,1)} reshape(bf16[64,64,256]{2,1,0:T(8,128)(2,1)S(1)} %gather_fusion.1) | data formatting | bytes 4194304 | tf_op jit(solution)/shard_map/reshape | solution.py:53
  19.3 2.0 %fusion = f32[4,2,16,128]{3,2,1,0:T(8,128)S(1)} fusion(bf16[4,1024,2,128]{3,2,1,0:T(2,128)(2,1)} %reshape.97, f32[4,2,1024,16]{2,3,1,0:T(8,128)S(1)} %get-tuple-element.22, f32[4,2,16]{2,1,0:T(2,128)S(1)} %get-tuple-element.21, pred[4,1024]{1,0:T(4,128)(4,1)S(1)} %broadcast_compare_fusion), kind=kOutput, calls=%fused_computation.2 | convolution fusion | flops 33947648 | bytes 2691584 | tf_op jit(solution)/shard_map/rkgs,rskd->rkgd/dot_general | solution.py:64
  21.3 3.8 %all-gather = f32[8,2,16,128]{3,2,1,0:T(8,128)S(1)} all-gather(f32[4,2,16,128]{3,2,1,0:T(8,128)S(1)} %fusion), channel_id=2, replica_groups=mesh['replica'=4,'kvhead'=4,'ffn'=2] {'ffn'}, dimensions={0}, use_global_device_ids=true | all-gather | bytes 196608 | tf_op jit(solution)/shard_map/all_gather | solution.py:15
  25.1 0.1 fusion.16
  25.3 9.3 %all-gather.3 = bf16[4,4,4096]{2,1,0:T(4,128)(2,1)S(1)} all-gather(bf16[1,4,4096]{2,1,0:T(4,128)(2,1)S(1)} %reshape.139), channel_id=1, replica_groups=mesh['replica'=4,'kvhead'=4,'ffn'=2] {'replica'}, dimensions={0}, use_global_device_ids=true | all-gather | bytes 163840 | tf_op jit(solution)/shard_map/all_gather | solution.py:77
  34.6 0.0 copy-start.3
  34.6 0.0 copy-start.4
  34.6 8.1 %fusion.23 = f32[16,2048]{1,0:T(8,128)S(1)} fusion(bf16[16,4096]{1,0:T(8,128)(2,1)S(1)} %reshape.140, bf16[4096,2048]{1,0:T(8,128)(2,1)} %param.15), kind=kOutput, calls=%fused_computation.41 | convolution fusion | flops 268435456 | bytes 17039360 | tf_op jit(solution)/shard_map/dot_general | solution.py:76
  42.7 0.0 copy-done.3
  42.7 17.8 %all-reduce.1 = bf16[16,2048]{1,0:T(8,128)(2,1)S(1)} all-reduce(f32[16,2048]{1,0:T(8,128)S(1)} %add_dynamic-update-slice_fusion), channel_id=1, replica_groups=mesh['replica'=4,'kvhead'=4,'ffn'=2] {'kvhead'}, use_global_device_ids=true, to_apply=%region_2.3 | all-reduce | flops 32768 | bytes 196608 | tf_op jit(solution)/shard_map/psum | solution.py:88
  60.5 0.1 fusion.11
  60.6 17.2 %psum.15 = f32[16]{0:T(128)S(1)} all-reduce(f32[16]{0:T(128)S(1)} %fusion.11), channel_id=1, replica_groups=mesh['replica'=4,'kvhead'=4,'ffn'=2] {'replica','ffn'}, use_global_device_ids=true, to_apply=%region_4.5 | all-reduce | flops 16 | bytes 128 | tf_op jit(solution)/shard_map/psum | solution.py:92
  77.8 0.0 copy-done.4
  77.8 0.1 fusion.13
  77.9 17.4 %all_gather.31 = bf16[16,16384]{1,0:T(8,128)(2,1)S(1)} all-gather(bf16[16,2048]{1,0:T(8,128)(2,1)S(1)} %fusion.13), channel_id=1, replica_groups=mesh['replica'=4,'kvhead'=4,'ffn'=2] {'replica','ffn'}, dimensions={1}, use_global_device_ids=true | all-gather | bytes 589824 | tf_op jit(solution)/shard_map/all_gather | solution.py:95
  95.3 12.4 %fusion.24 = f32[16,832]{1,0:T(8,128)S(1)} fusion(bf16[16,16384]{1,0:T(8,128)(2,1)S(1)} %all_gather.31, bf16[832,16384]{1,0:T(8,128)(2,1)} %param.18), kind=kOutput, calls=%fused_computation.42 | convolution fusion | flops 436207616 | bytes 27840512 | tf_op jit(solution)/shard_map/dot_general | solution.py:96
  107.7 13.2 %fusion.7 = bf16[16,832]{1,0:T(8,128)(2,1)} fusion(bf16[16,16384]{1,0:T(8,128)(2,1)S(1)} %all_gather.31, bf16[832,16384]{1,0:T(8,128)(2,1)} %param.19, f32[16,832]{1,0:T(8,128)S(1)} %fusion.24), kind=kOutput, calls=%fused_computation.8 | convolution fusion | flops 436287488 | bytes 27867136 | tf_op jit(solution)/shard_map/dot_general | solution.py:99
  120.9 0.6 constant_dynamic-slice_fusion
  121.5 0.0 copy-done.1
  (11 shorter events, 0.1 us)
Async XLA Ops:
  0.6 1.7 %copy-start = (bf16[64,64,256]{2,1,0:T(8,128)(2,1)S(1)}, bf16[64,64,256]{2,1,0:T(8,128)(2,1)}, u32[]{:S(2)}) copy-start(bf16[64,64,256]{2,1,0:T(8,128)(2,1)} %param.11) | copy-start | bytes 6291460
  4.4 2.6 %copy-start.2 = (bf16[4,4096]{1,0:T(4,128)(2,1)S(1)}, bf16[4,4096]{1,0:T(4,128)(2,1)}, u32[]{:S(2)}) copy-start(bf16[4,4096]{1,0:T(4,128)(2,1)} %param.10) | copy-start | bytes 98308
  34.6 8.1 %copy-start.3 = (bf16[4,2048]{1,0:T(4,128)(2,1)S(1)}, bf16[4,2048]{1,0:T(4,128)(2,1)}, u32[]{:S(2)}) copy-start(bf16[4,2048]{1,0:T(4,128)(2,1)} %param.16) | copy-start | bytes 49156
  34.6 43.2 %copy-start.4 = (bf16[2048]{0:T(1024)(128)(2,1)S(1)}, bf16[2048]{0:T(1024)(128)(2,1)}, u32[]{:S(2)}) copy-start(bf16[2048]{0:T(1024)(128)(2,1)} %param.17) | copy-start | bytes 12292
  107.7 13.8 %copy-start.1 = (bf16[64,64,256]{2,1,0:T(8,128)(2,1)S(1)}, bf16[64,64,256]{2,1,0:T(8,128)(2,1)}, u32[]{:S(2)}) copy-start(bf16[64,64,256]{2,1,0:T(8,128)(2,1)} %param.11) | copy-start | bytes 6291460
where the time goes:
time: 122 us; the launch traced here: 121 us
  blocking collectives  72.4 us (59%)
  matrix products  36.4 us (30%)
  local copies, waits for them, and re-layouts  9.74 us (8%)
  other arithmetic  2.21 us (2%)
    psum x1, blocking collectives, per_device(): summed = lax.psum(partial_value, 'kvhead')  17.8 us
    all_gather x1, blocking collectives, per_device(): shard_cols = lax.all_gather(normed, ('replica', 'ffn'), axis=1, tiled=True)  17.4 us
    psum x1, blocking collectives, per_device(): squares = lax.psum(jnp.sum(widened * widened, axis=1), ('replica', 'ffn'))  17.2 us
    dot_general x1, matrix products, per_device(): lax.dot_general(shard_cols, up_weight, contract, preferred_element_type=j...  13.2 us
    dot_general x1, matrix products, per_device(): lax.dot_general(shard_cols, gate_weight, contract, preferred_element_type...  12.4 us
    all_gather x3, blocking collectives, merged(): gathered = jax.tree.map(lambda a: lax.all_gather(a, axis), part)  10.7 us
    all_gather x1, blocking collectives, per_device(): lax.all_gather(contexts, 'replica', axis=0, tiled=True)  9.29 us
    dot_general x1, matrix products, per_device(): jnp.dot(lax.all_gather(contexts, 'replica', axis=0, tiled=True), out_proj...  8.05 us

commit v1 on v0

--- a/solution.py
+++ b/solution.py
@@ -85,7 +85,9 @@
     )
     partial_value = lax.dynamic_update_slice_in_dim(partial_value, own_part, own_first, 0)
     gain_wide = norm_gain.astype(jnp.float32)
-    summed = lax.psum(partial_value, "kvhead")
+    summed = partial_value
+    for hop in (1, 2):
+        summed = summed + lax.ppermute(summed, "kvhead", [(dev, dev ^ hop) for dev in range(4)])
     post_all = summed.astype(jnp.bfloat16)
     post_attn = lax.dynamic_slice_in_dim(post_all, own_first, own_count, 0)
     widened = post_all.astype(jnp.float32)

time: 122 us -> 115 us (0.943)
  blocking collectives: 72.4 us -> 51.8 us
  waiting for transfers between devices: 0 us -> 9.46 us
  starting transfers between devices: 0 us -> 4.07 us
    psum x1 -> x0, blocking collectives: 17.8 us -> none  [per_device(): summed = lax.psum(partial_value, 'kvhead')]
    ppermute x0 -> x2, waiting for transfers between devices: none -> 9.46 us  [per_device(): lax.ppermute(summed, 'kvhead', [(dev, dev ^ hop) for dev in range(4)])]
    ppermute x0 -> x2, starting transfers between devices: none -> 4.07 us  [per_device(): lax.ppermute(summed, 'kvhead', [(dev, dev ^ hop) for dev in range(4)])]
    psum x1, blocking collectives: 17.2 us -> 14.4 us  [per_device(): squares = lax.psum(jnp.sum(widened * widened, axis=1), ('replica', 'ffn'))]
  transfers between devices with their start and end apart: 0 -> 2, of which waited for: 0 -> 2; matrix products, arithmetic and copies ran while one was open for 0% -> 0% of each run, Pallas kernels for 0% -> 0%
where the time goes in v1:
time: 115 us; the launch traced here: 114 us
  blocking collectives  51.8 us (45%)
  matrix products  36.4 us (32%)
  local copies, waits for them, and re-layouts  10.4 us (9%)
  waiting for transfers between devices  9.46 us (8%)
  starting transfers between devices  4.07 us (4%)
  other arithmetic  1.56 us (1%)
    all_gather x1, blocking collectives, per_device(): shard_cols = lax.all_gather(normed, ('replica', 'ffn'), axis=1, tiled=True)  17.4 us
    psum x1, blocking collectives, per_device(): squares = lax.psum(jnp.sum(widened * widened, axis=1), ('replica', 'ffn'))  14.4 us
    dot_general x1, matrix products, per_device(): lax.dot_general(shard_cols, up_weight, contract, preferred_element_type=j...  13.2 us
    dot_general x1, matrix products, per_device(): lax.dot_general(shard_cols, gate_weight, contract, preferred_element_type...  12.4 us
    all_gather x3, blocking collectives, merged(): gathered = jax.tree.map(lambda a: lax.all_gather(a, axis), part)  10.7 us
    ppermute x2, waiting for transfers between devices, per_device(): lax.ppermute(summed, 'kvhead', [(dev, dev ^ hop) for dev in range(4)])  9.46 us
    all_gather x1, blocking collectives, per_device(): lax.all_gather(contexts, 'replica', axis=0, tiled=True)  9.29 us
    dot_general x1, matrix products, per_device(): jnp.dot(lax.all_gather(contexts, 'replica', axis=0, tiled=True), out_proj...  8.05 us
  transfers between devices with their start and end apart: 2, of which 2 were waited for; matrix products, arithmetic and copies ran while one was open for 0% of the time, Pallas kernels for 0%

profile of v1, /device:TPU:1, one launch (start us, length us, event | category | flops | bytes accessed | tf_op | source)
XLA Modules:
  0.0 114.5 jit_solution(1354989917903433492)
XLA Ops:
  0.6 0.0 copy-start
  0.7 0.8 compare_select_fusion
  1.5 0.1 reshape.100
  1.6 0.7 copy-done
  2.2 2.0 %gather_fusion = bf16[64,64,256]{2,1,0:T(8,128)(2,1)} fusion(bf16[64,64,256]{2,1,0:T(8,128)(2,1)S(1)} %copy-done, s32[1024]{0:T(1024)S(1)} %pad_clamp_fusion), kind=kCustom, calls=%fused_computation | custom fusion | bytes 4194560 | tf_op jit(solution)/shard_map/gather | solution.py:52
  4.3 2.6 %reshape.95 = bf16[4,1024,2,128]{3,2,1,0:T(2,128)(2,1)S(1)} reshape(bf16[64,64,256]{2,1,0:T(8,128)(2,1)} %gather_fusion) | data formatting | bytes 4194304 | tf_op jit(solution)/shard_map/reshape | solution.py:52
  6.8 0.0 copy-done.2
  6.9 0.1 broadcast_compare_fusion
  7.0 0.7 select_reduce_fusion
  7.7 3.8 %all-gather.1 = f32[8,2,16]{2,1,0:T(2,128)S(1)} all-gather(f32[4,2,16]{2,1,0:T(2,128)S(1)} %get-tuple-element.23), channel_id=3, replica_groups=mesh['replica'=4,'kvhead'=4,'ffn'=2] {'ffn'}, dimensions={0}, use_global_device_ids=true | all-gather | bytes 1536 | tf_op jit(solution)/shard_map/all_gather | solution.py:15
  11.5 0.2 bitcast_reduce_fusion
  11.7 3.2 %all-gather.2 = f32[8,2,16]{2,1,0:T(2,128)S(1)} all-gather(f32[4,2,16]{2,1,0:T(2,128)S(1)} %bitcast_reduce_fusion), channel_id=4, replica_groups=mesh['replica'=4,'kvhead'=4,'ffn'=2] {'ffn'}, dimensions={0}, use_global_device_ids=true | all-gather | bytes 1536 | tf_op jit(solution)/shard_map/all_gather | solution.py:15
  14.9 2.3 %gather_fusion.1 = bf16[64,64,256]{2,1,0:T(8,128)(2,1)S(1)} fusion(bf16[64,64,256]{2,1,0:T(8,128)(2,1)} %param.12, s32[1024]{0:T(1024)S(1)} %pad_clamp_fusion), kind=kCustom, calls=%fused_computation.1 | custom fusion | bytes 4194560 | tf_op jit(solution)/shard_map/gather | solution.py:53
  17.2 2.1 %reshape.97 = bf16[4,1024,2,128]{3,2,1,0:T(2,128)(2,1)} reshape(bf16[64,64,256]{2,1,0:T(8,128)(2,1)S(1)} %gather_fusion.1) | data formatting | bytes 4194304 | tf_op jit(solution)/shard_map/reshape | solution.py:53
  19.3 2.0 %fusion = f32[4,2,16,128]{3,2,1,0:T(8,128)S(1)} fusion(bf16[4,1024,2,128]{3,2,1,0:T(2,128)(2,1)} %reshape.97, f32[4,2,1024,16]{2,3,1,0:T(8,128)S(1)} %get-tuple-element.32, f32[4,2,16]{2,1,0:T(2,128)S(1)} %get-tuple-element.23, pred[4,1024]{1,0:T(4,128)(4,1)S(1)} %broadcast_compare_fusion), kind=kOutput, calls=%fused_computation.2 | convolution fusion | flops 33947648 | bytes 2691584 | tf_op jit(solution)/shard_map/rkgs,rskd->rkgd/dot_general | solution.py:64
  21.3 3.8 %all-gather = f32[8,2,16,128]{3,2,1,0:T(8,128)S(1)} all-gather(f32[4,2,16,128]{3,2,1,0:T(8,128)S(1)} %fusion), channel_id=2, replica_groups=mesh['replica'=4,'kvhead'=4,'ffn'=2] {'ffn'}, dimensions={0}, use_global_device_ids=true | all-gather | bytes 196608 | tf_op jit(solution)/shard_map/all_gather | solution.py:15
  25.1 0.1 fusion.16
  25.3 9.3 %all-gather.3 = bf16[4,4,4096]{2,1,0:T(4,128)(2,1)S(1)} all-gather(bf16[1,4,4096]{2,1,0:T(4,128)(2,1)S(1)} %reshape.139), channel_id=1, replica_groups=mesh['replica'=4,'kvhead'=4,'ffn'=2] {'replica'}, dimensions={0}, use_global_device_ids=true | all-gather | bytes 163840 | tf_op jit(solution)/shard_map/all_gather | solution.py:77
  34.6 0.0 copy-start.3
  34.6 0.0 copy-start.4
  34.6 8.1 %fusion.23 = f32[16,2048]{1,0:T(8,128)S(1)} fusion(bf16[16,4096]{1,0:T(8,128)(2,1)S(1)} %reshape.140, bf16[4096,2048]{1,0:T(8,128)(2,1)} %param.15), kind=kOutput, calls=%fused_computation.42 | convolution fusion | flops 268435456 | bytes 17039360 | tf_op jit(solution)/shard_map/dot_general | solution.py:76
  42.7 1.7 %collective-permute-start = (f32[16,2048]{1,0:T(8,128)S(1)}, f32[16,2048]{1,0:T(8,128)S(1)}, u32[]{:S(2)}, u32[]{:S(2)}) collective-permute-start(f32[16,2048]{1,0:T(8,128)S(1)} %add_dynamic-update-slice_fusion), channel_id=1, source_target_pairs={{0,2},{2,0},{4,6},{6,4},{1,3},{3,1},{5,7},{7,5},{8,10},{10,8},{12,... | collective-permute-start | bytes 393224 | tf_op jit(solution)/shard_map/ppermute | solution.py:90
  44.4 3.6 %collective-permute-done = f32[16,2048]{1,0:T(8,128)S(1)} collective-permute-done((f32[16,2048]{1,0:T(8,128)S(1)}, f32[16,2048]{1,0:T(8,128)S(1)}, u32[]{:S(2)}, u32[]{:S(2)}) %collective-permute-start) | collective-permute-done | bytes 131104 | tf_op jit(solution)/shard_map/ppermute | solution.py:90
  48.1 2.4 %collective-permute-start.1 = (f32[16,2048]{1,0:T(8,128)S(1)}, f32[16,2048]{1,0:T(8,128)S(1)}, u32[]{:S(2)}, u32[]{:S(2)}) collective-permute-start(f32[16,2048]{1,0:T(8,128)S(1)} %add.70), channel_id=1, source_target_pairs={{0,4},{2,6},{4,0},{6,2},{1,5},{3,7},{5,1},{7,3},{8,12},{10,14},{12... | collective-permute-start | bytes 393224 | tf_op jit(solution)/shard_map/ppermute | solution.py:90
  50.4 5.8 %collective-permute-done.1 = f32[16,2048]{1,0:T(8,128)S(1)} collective-permute-done((f32[16,2048]{1,0:T(8,128)S(1)}, f32[16,2048]{1,0:T(8,128)S(1)}, u32[]{:S(2)}, u32[]{:S(2)}) %collective-permute-start.1) | collective-permute-done | bytes 131104 | tf_op jit(solution)/shard_map/ppermute | solution.py:90
  56.3 0.1 fusion.11
  56.4 14.4 %psum.7 = f32[16]{0:T(128)S(1)} all-reduce(f32[16]{0:T(128)S(1)} %get-tuple-element.18), channel_id=1, replica_groups=mesh['replica'=4,'kvhead'=4,'ffn'=2] {'replica','ffn'}, use_global_device_ids=true, to_apply=%region_3.4 | all-reduce | flops 16 | bytes 128 | tf_op jit(solution)/shard_map/psum | solution.py:94
  70.8 0.6 constant_dynamic-slice_fusion
  71.4 0.1 fusion.13
  71.5 17.4 %all_gather.31 = bf16[16,16384]{1,0:T(8,128)(2,1)S(1)} all-gather(bf16[16,2048]{1,0:T(8,128)(2,1)S(1)} %fusion.13), channel_id=1, replica_groups=mesh['replica'=4,'kvhead'=4,'ffn'=2] {'replica','ffn'}, dimensions={1}, use_global_device_ids=true | all-gather | bytes 589824 | tf_op jit(solution)/shard_map/all_gather | solution.py:97
  88.9 12.4 %fusion.24 = f32[16,832]{1,0:T(8,128)S(1)} fusion(bf16[16,16384]{1,0:T(8,128)(2,1)S(1)} %all_gather.31, bf16[832,16384]{1,0:T(8,128)(2,1)} %param.18), kind=kOutput, calls=%fused_computation.43 | convolution fusion | flops 436207616 | bytes 27840512 | tf_op jit(solution)/shard_map/dot_general | solution.py:98
  101.3 13.2 %fusion.7 = bf16[16,832]{1,0:T(8,128)(2,1)} fusion(bf16[16,16384]{1,0:T(8,128)(2,1)S(1)} %all_gather.31, bf16[832,16384]{1,0:T(8,128)(2,1)} %param.19, f32[16,832]{1,0:T(8,128)S(1)} %fusion.24), kind=kOutput, calls=%fused_computation.8 | convolution fusion | flops 436287488 | bytes 27867136 | tf_op jit(solution)/shard_map/dot_general | solution.py:101
  (17 shorter events, 0.2 us)
Async XLA Ops:
  0.6 1.6 %copy-start = (bf16[64,64,256]{2,1,0:T(8,128)(2,1)S(1)}, bf16[64,64,256]{2,1,0:T(8,128)(2,1)}, u32[]{:S(2)}) copy-start(bf16[64,64,256]{2,1,0:T(8,128)(2,1)} %param.11) | copy-start | bytes 6291460
  4.3 2.6 %copy-start.2 = (bf16[4,4096]{1,0:T(4,128)(2,1)S(1)}, bf16[4,4096]{1,0:T(4,128)(2,1)}, u32[]{:S(2)}) copy-start(bf16[4,4096]{1,0:T(4,128)(2,1)} %param.10) | copy-start | bytes 98308
  4.3 2.6 %copy-start.5 = (s32[4]{0:T(128)S(1)}, s32[4]{0:T(128)}, u32[]{:S(2)}) copy-start(s32[4]{0:T(128)} %param.14) | copy-start | bytes 52
  34.6 8.1 %copy-start.3 = (bf16[4,2048]{1,0:T(4,128)(2,1)S(1)}, bf16[4,2048]{1,0:T(4,128)(2,1)}, u32[]{:S(2)}) copy-start(bf16[4,2048]{1,0:T(4,128)(2,1)} %param.16) | copy-start | bytes 49156
  34.6 15.8 %copy-start.4 = (bf16[2048]{0:T(1024)(128)(2,1)S(1)}, bf16[2048]{0:T(1024)(128)(2,1)}, u32[]{:S(2)}) copy-start(bf16[2048]{0:T(1024)(128)(2,1)} %param.17) | copy-start | bytes 12292
  42.7 5.3 %collective-permute-start = (f32[16,2048]{1,0:T(8,128)S(1)}, f32[16,2048]{1,0:T(8,128)S(1)}, u32[]{:S(2)}, u32[]{:S(2)}) collective-permute-start(f32[16,2048]{1,0:T(8,128)S(1)} %add_dynamic-update-slice_fusion), channel_id=1, source_target_pairs={{0,2},{2,0},{4,6},{6,4},{1,3},{3,1},{5,7},{7,5},{8,10},{10,8},{12,... | collective-permute-start | bytes 393224 | tf_op jit(solution)/shard_map/ppermute | solution.py:90
  48.1 8.2 %collective-permute-start.1 = (f32[16,2048]{1,0:T(8,128)S(1)}, f32[16,2048]{1,0:T(8,128)S(1)}, u32[]{:S(2)}, u32[]{:S(2)}) collective-permute-start(f32[16,2048]{1,0:T(8,128)S(1)} %add.70), channel_id=1, source_target_pairs={{0,4},{2,6},{4,0},{6,2},{1,5},{3,7},{5,1},{7,3},{8,12},{10,14},{12... | collective-permute-start | bytes 393224 | tf_op jit(solution)/shard_map/ppermute | solution.py:90
  101.3 13.2 %copy-start.1 = (bf16[64,64,256]{2,1,0:T(8,128)(2,1)S(1)}, bf16[64,64,256]{2,1,0:T(8,128)(2,1)}, u32[]{:S(2)}) copy-start(bf16[64,64,256]{2,1,0:T(8,128)(2,1)} %param.11) | copy-start | bytes 6291460
